TPU v7x, 512 devices: a whole 4x4x16 slice. The times are simulated.
512 devices in a mesh: grp: 8 (over x, core), wide: 64 (over z, y).
Axes of the slice: x: 4, y: 4, z: 16, core: 2. Of those that a mesh axis runs over, the one named last changes fastest.
Arguments:
- anchor_states: bfloat16 [65536, 1024], P(('wide', 'grp')), may hold values from -6 to 6
- key_weight: bfloat16 [1024, 1024], P(None, 'grp'), may hold values from -0.1875 to 0.1875
- value_weight: bfloat16 [1024, 1024], P(None, 'grp'), may hold values from -0.1875 to 0.1875
- panel_query: bfloat16 [131072, 1024], P(('wide', 'grp')), may hold values from -160 to 160
- cell_list: int32 [1024, 4], P('wide'), may hold values from 0 to 7, as said below
- cell_count: int32 [1024], P('wide'), may hold values from 1 to 4, as said below
- norm_gain: float32 [1024], replicated, may hold values from 0.1 to 1.9
- up_weight: bfloat16 [1024, 512], replicated, may hold values from -0.1875 to 0.1875
- flux_weight: bfloat16 [4, 512], replicated, may hold values from -0.25 to 0.25
Outputs:
- flux: float32 [4, 131072], P(None, ('wide', 'grp'))
Inputs may be any that keep to these rules, and one draw needn't show every extreme that they name: `cell_list`: the entries of a row are distinct cell blocks of that panel block's region; entries past cell_count are not used. `cell_count`: every region has a panel block whose list uses all 4 slots.
All inputs are finite; a program needn't handle non-finite values.
Results may differ from a plain program's by a relative error of at most 0.007.
Values may be sent and summed in bfloat16 or wider, within the bound.
No kernel may reach another device: no remote copies, remote signals or barrier semaphores. Data moves between devices by JAX's collectives and lax.ppermute only.
A program may use at most 64 MiB of HBM per device.

v0:
```python
import math
import jax
import jax.numpy as jnp
from jax import lax
from jax.sharding import PartitionSpec as P

BLK = 128
LMAX = 4
HD = 64


def softmax_rows(scores, mask):
    scores = jnp.where(mask[:, None, None, :], scores, -jnp.inf)
    top = jnp.max(scores, axis=-1, keepdims=True)
    expo = jnp.exp(scores - top)
    return (expo / jnp.sum(expo, axis=-1, keepdims=True)).astype(jnp.bfloat16)


def wall_flux(query_rows, attended_rows, norm_gain, up_weight, flux_weight):
    stream = query_rows.astype(jnp.float32) + attended_rows.astype(jnp.float32)
    scale = lax.rsqrt(jnp.mean(stream * stream, axis=-1, keepdims=True) + 1e-06)
    normed = (stream * scale * norm_gain[None, :]).astype(jnp.bfloat16)
    hidden = jax.nn.gelu(jnp.dot(normed, up_weight, preferred_element_type=jnp.float32)).astype(
        jnp.bfloat16
    )
    return lax.dot_general(
        flux_weight, hidden, (((1,), (1,)), ((), ())), preferred_element_type=jnp.float32
    )


def body(
    anchor_states,
    key_weight,
    value_weight,
    panel_query,
    cell_list,
    cell_count,
    norm_gain,
    up_weight,
    flux_weight,
):
    full_keys_w, full_values_w = (
        lax.all_gather(key_weight, "grp", axis=1, tiled=True),
        lax.all_gather(value_weight, "grp", axis=1, tiled=True),
    )
    local_keys = jnp.dot(anchor_states, full_keys_w, preferred_element_type=jnp.float32).astype(
        jnp.bfloat16
    )
    local_values = jnp.dot(anchor_states, full_values_w, preferred_element_type=jnp.float32).astype(
        jnp.bfloat16
    )
    region_keys, region_values = (
        lax.all_to_all(local_keys, "grp", split_axis=1, concat_axis=0, tiled=True),
        lax.all_to_all(local_values, "grp", split_axis=1, concat_axis=0, tiled=True),
    )
    region_query = lax.all_to_all(
        lax.all_to_all(panel_query, "grp", split_axis=1, concat_axis=0, tiled=True),
        "wide",
        split_axis=0,
        concat_axis=0,
        tiled=True,
    )
    local_heads = region_keys.shape[1] // HD
    cell_blocks = region_keys.shape[0] // BLK
    block_count = region_query.shape[0] // BLK
    per_step = math.gcd(block_count, 4)
    steps = block_count // per_step
    key_blocks = region_keys.reshape(cell_blocks, BLK, local_heads, HD)
    value_blocks = region_values.reshape(cell_blocks, BLK, local_heads, HD)
    query_groups = region_query.reshape(steps, per_step, BLK, local_heads, HD)
    list_groups = cell_list.reshape(steps, per_step, LMAX)
    count_groups = cell_count.reshape(steps, per_step)
    slot_index = jnp.arange(LMAX, dtype=jnp.int32)

    def attend(item):
        query_group, listed, counts = item
        live = slot_index[None, :] < counts[:, None]
        picked_keys = key_blocks[listed].reshape(per_step, LMAX * BLK, local_heads, HD)
        picked_values = value_blocks[listed].reshape(per_step, LMAX * BLK, local_heads, HD)
        mask = jnp.repeat(live, BLK, axis=1)
        scores = jnp.einsum(
            "bihd,bjhd->bhij", query_group, picked_keys, preferred_element_type=jnp.float32
        ) / math.sqrt(HD)
        weights = softmax_rows(scores, mask)
        output = jnp.einsum(
            "bhij,bjhd->bihd", weights, picked_values, preferred_element_type=jnp.float32
        )
        return output.astype(jnp.bfloat16)

    attended = lax.map(attend, (query_groups, list_groups, count_groups))
    attended = attended.reshape(block_count * BLK, local_heads * HD)
    panel_rows = lax.all_to_all(
        lax.all_to_all(attended, "wide", split_axis=0, concat_axis=0, tiled=True),
        "grp",
        split_axis=0,
        concat_axis=1,
        tiled=True,
    )
    return wall_flux(panel_query, panel_rows, norm_gain, up_weight, flux_weight)


def solution(mesh):
    in_specs = (
        P(("wide", "grp"), None),
        P(None, "grp"),
        P(None, "grp"),
        P(("wide", "grp"), None),
        P("wide", None),
        P("wide"),
        P(),
        P(),
        P(),
    )
    out_specs = P(None, ("wide", "grp"))
    return jax.shard_map(body, mesh=mesh, in_specs=in_specs, out_specs=out_specs, check_vma=False)
```

profile of v0, /device:TPU:1, one launch (start us, length us, event | category | flops | bytes accessed | tf_op | source)
XLA Modules:
  0.0 225.5 jit_solution(5993352546024872910)
XLA Ops:
  9.3 18.6 %all_to_all.79 = bf16[256,8,128]{0,2,1:T(8,128)(2,1)S(1)} all-to-all(bf16[256,8,128]{0,2,1:T(8,128)(2,1)S(1)} %bitcast.78), channel_id=1, replica_groups=mesh['grp'=8,'wide'=64] {'grp'}, dimensions={1} | all-to-all | bytes 1048576 | tf_op jit(solution)/shard_map/all_to_all | solution.py:57
  29.0 14.8 %all-to-all-start.2 = ((bf16[64,32,128]{2,1,0:T(8,128)(2,1)}), bf16[64,32,128]{2,1,0:T(8,128)(2,1)S(1)}, u32[]{:S(2)}, u32[]{:S(2)}) async-start(bf16[64,32,128]{2,1,0:T(8,128)(2,1)} %bitcast.6), calls=%async_computation.2 | async-start | bytes 1048576 | tf_op jit(solution)/shard_map/all_to_all | solution.py:56
  43.7 6.4 %all-gather.3.cloned.1.call-done = bf16[1024,1024]{1,0:T(8,128)(2,1)} async-done(((bf16[1024,128]{1,0:T(8,128)(2,1)}), bf16[1024,1024]{1,0:T(8,128)(2,1)}) %all-gather.3.cloned.1.call-update) | async-done | bytes 2097168 | tf_op jit(solution)/shard_map/all_gather | solution.py:44
  50.1 2.0 convolution_convert_fusion.2
  53.0 19.9 %all-to-all-done.2 = bf16[64,32,128]{2,1,0:T(8,128)(2,1)S(1)} async-done(((bf16[64,32,128]{2,1,0:T(8,128)(2,1)}), bf16[64,32,128]{2,1,0:T(8,128)(2,1)S(1)}, u32[]{:S(2)}, u32[]{:S(2)}) %all-to-all-start.2) | async-done | bytes 524320 | tf_op jit(solution)/shard_map/all_to_all | solution.py:56
  72.9 8.1 %all-to-all-start = ((bf16[128,8,128]{0,2,1:T(8,128)(2,1)}), bf16[128,8,128]{0,2,1:T(8,128)(2,1)S(1)}, u32[]{:S(2)}, u32[]{:S(2)}) async-start(bf16[128,8,128]{0,2,1:T(8,128)(2,1)} %bitcast.1), calls=%async_computation | async-start | bytes 524288 | tf_op jit(solution)/shard_map/all_to_all | solution.py:54
  81.0 10.1 %all-gather.5.cloned.1.call-done = bf16[1024,1024]{1,0:T(8,128)(2,1)} async-done(((bf16[1024,128]{1,0:T(8,128)(2,1)}), bf16[1024,1024]{1,0:T(8,128)(2,1)}) %all-gather.5.cloned.1.call-update) | async-done | bytes 2097168 | tf_op jit(solution)/shard_map/all_gather | solution.py:43
  91.1 2.0 convolution_convert_fusion.1
  93.9 4.2 %all-to-all-start.3 = ((bf16[128,8,128]{0,2,1:T(8,128)(2,1)}), bf16[128,8,128]{0,2,1:T(8,128)(2,1)S(1)}, u32[]{:S(2)}, u32[]{:S(2)}) async-start(bf16[128,8,128]{0,2,1:T(8,128)(2,1)} %bitcast.7), calls=%async_computation.3 | async-start | bytes 524288 | tf_op jit(solution)/shard_map/all_to_all | solution.py:53
  98.8 1.8 copy.33
  100.9 3.8 %all-to-all-done.3 = bf16[128,8,128]{0,2,1:T(8,128)(2,1)S(1)} async-done(((bf16[128,8,128]{0,2,1:T(8,128)(2,1)}), bf16[128,8,128]{0,2,1:T(8,128)(2,1)S(1)}, u32[]{:S(2)}, u32[]{:S(2)}) %all-to-all-start.3) | async-done | bytes 262176 | tf_op jit(solution)/shard_map/all_to_all | solution.py:53
  105.1 46.4 %while.11 = (s32[]{:T(128)}, bf16[4,4,128,2,64]{2,4,3,1,0:T(8,128)(2,1)}, s32[4,4,4]{2,1,0:T(4,128)S(1)}, bf16[8,128,2,64]{3,2,1,0:T(2,128)(2,1)S(1)}, s32[4,4]{...) while((s32[]{:T(128)}, ...), condition=%wide.region_3.4_spmd.clone, body=%wide.region_0.3_spmd.clone.sunk | while | flops 137430592 | bytes 7624301 | solution.py:90
  105.2 2.7 %gather_fusion.1 = bf16[16,128,2,64]{3,2,1,0:T(2,128)(2,1)S(1)} fusion(bf16[8,128,2,64]{3,2,1,0:T(2,128)(2,1)S(1)} %get-tuple-element.170, s32[1024]{0:T(1024)S(1)} %pad_clamp_fusion.2), kind=kCustom, calls=%fused_computation.1.clone.clone.1 | custom fusion | bytes 1048640 | tf_op jit(solution)/shard_map/while/body/eval_jaxpr/gather | solution.py:78
  108.1 3.1 %fusion.69 = (f32[4,2,128]{2,1,0:T(2,128)S(1)}, f32[4,2,128,512]{3,2,1,0:T(8,128)}) fusion(pred[4,512]{1,0:T(4,128)(4,1)S(1)} %bitcast.83, bf16[4,512,2,64]{3,2,1,0:T(2,128)(2,1)S(1)} %bitcast.76, bf16[4,4,128,2,64]{2,4,3,1,0:T(8,128)(2,1)} %get-tuple-element.169, s32[]{:T(128)} %get-tuple-element.156), kind=kOutput, calls=%fused_computation.51.clone.1 | convolution fusion | flops 69206528 | bytes 2759168 | tf_op jit(solution)/shard_map/while/body/eval_jaxpr/sub | solution.py:15
  111.1 2.7 %gather_fusion = bf16[16,128,2,64]{3,2,1,0:T(2,128)(2,1)S(1)} fusion(bf16[8,128,2,64]{3,2,1,0:T(2,128)(2,1)S(1)} %get-tuple-element.167, s32[1024]{0:T(1024)S(1)} %pad_clamp_fusion.2), kind=kCustom, calls=%fused_computation.clone.clone.1 | custom fusion | bytes 1048640 | tf_op jit(solution)/shard_map/while/body/eval_jaxpr/gather | solution.py:79
  113.8 2.9 %fusion.70 = bf16[4,4,128,2,64]{2,4,3,1,0:T(8,128)(2,1)} fusion(bf16[4,4,128,2,64]{2,4,3,1,0:T(8,128)(2,1)} %get-tuple-element.157, s32[]{:T(128)} %get-tuple-element.156, bf16[4,512,2,64]{3,2,1,0:T(2,128)(2,1)S(1)} %bitcast.77, f32[4,2,128,512]{3,2,1,0:T(8,128)} %get-tuple-element.146, f32[4,2,128]{2,1,0:T(2,128)S(1)} %get-tuple-element.147), kind=kOutput, calls=%fused_computation.10.clone.1 | convolution fusion | flops 68222976 | bytes 2757120 | tf_op jit(solution)/shard_map/while/body/eval_jaxpr/bhij,bjhd->bihd/dot_general | solution.py:85
  116.8 2.7 %gather_fusion.1 = bf16[16,128,2,64]{3,2,1,0:T(2,128)(2,1)S(1)} fusion(bf16[8,128,2,64]{3,2,1,0:T(2,128)(2,1)S(1)} %get-tuple-element.170, s32[1024]{0:T(1024)S(1)} %pad_clamp_fusion.2), kind=kCustom, calls=%fused_computation.1.clone.clone.1 | custom fusion | bytes 1048640 | tf_op jit(solution)/shard_map/while/body/eval_jaxpr/gather | solution.py:78
  119.6 3.1 %fusion.69 = (f32[4,2,128]{2,1,0:T(2,128)S(1)}, f32[4,2,128,512]{3,2,1,0:T(8,128)}) fusion(pred[4,512]{1,0:T(4,128)(4,1)S(1)} %bitcast.83, bf16[4,512,2,64]{3,2,1,0:T(2,128)(2,1)S(1)} %bitcast.76, bf16[4,4,128,2,64]{2,4,3,1,0:T(8,128)(2,1)} %get-tuple-element.169, s32[]{:T(128)} %get-tuple-element.156), kind=kOutput, calls=%fused_computation.51.clone.1 | convolution fusion | flops 69206528 | bytes 2759168 | tf_op jit(solution)/shard_map/while/body/eval_jaxpr/sub | solution.py:15
  122.7 2.7 %gather_fusion = bf16[16,128,2,64]{3,2,1,0:T(2,128)(2,1)S(1)} fusion(bf16[8,128,2,64]{3,2,1,0:T(2,128)(2,1)S(1)} %get-tuple-element.167, s32[1024]{0:T(1024)S(1)} %pad_clamp_fusion.2), kind=kCustom, calls=%fused_computation.clone.clone.1 | custom fusion | bytes 1048640 | tf_op jit(solution)/shard_map/while/body/eval_jaxpr/gather | solution.py:79
  125.4 2.9 %fusion.70 = bf16[4,4,128,2,64]{2,4,3,1,0:T(8,128)(2,1)} fusion(bf16[4,4,128,2,64]{2,4,3,1,0:T(8,128)(2,1)} %get-tuple-element.157, s32[]{:T(128)} %get-tuple-element.156, bf16[4,512,2,64]{3,2,1,0:T(2,128)(2,1)S(1)} %bitcast.77, f32[4,2,128,512]{3,2,1,0:T(8,128)} %get-tuple-element.146, f32[4,2,128]{2,1,0:T(2,128)S(1)} %get-tuple-element.147), kind=kOutput, calls=%fused_computation.10.clone.1 | convolution fusion | flops 68222976 | bytes 2757120 | tf_op jit(solution)/shard_map/while/body/eval_jaxpr/bhij,bjhd->bihd/dot_general | solution.py:85
  128.4 2.7 %gather_fusion.1 = bf16[16,128,2,64]{3,2,1,0:T(2,128)(2,1)S(1)} fusion(bf16[8,128,2,64]{3,2,1,0:T(2,128)(2,1)S(1)} %get-tuple-element.170, s32[1024]{0:T(1024)S(1)} %pad_clamp_fusion.2), kind=kCustom, calls=%fused_computation.1.clone.clone.1 | custom fusion | bytes 1048640 | tf_op jit(solution)/shard_map/while/body/eval_jaxpr/gather | solution.py:78
  131.2 3.1 %fusion.69 = (f32[4,2,128]{2,1,0:T(2,128)S(1)}, f32[4,2,128,512]{3,2,1,0:T(8,128)}) fusion(pred[4,512]{1,0:T(4,128)(4,1)S(1)} %bitcast.83, bf16[4,512,2,64]{3,2,1,0:T(2,128)(2,1)S(1)} %bitcast.76, bf16[4,4,128,2,64]{2,4,3,1,0:T(8,128)(2,1)} %get-tuple-element.169, s32[]{:T(128)} %get-tuple-element.156), kind=kOutput, calls=%fused_computation.51.clone.1 | convolution fusion | flops 69206528 | bytes 2759168 | tf_op jit(solution)/shard_map/while/body/eval_jaxpr/sub | solution.py:15
  134.3 2.7 %gather_fusion = bf16[16,128,2,64]{3,2,1,0:T(2,128)(2,1)S(1)} fusion(bf16[8,128,2,64]{3,2,1,0:T(2,128)(2,1)S(1)} %get-tuple-element.167, s32[1024]{0:T(1024)S(1)} %pad_clamp_fusion.2), kind=kCustom, calls=%fused_computation.clone.clone.1 | custom fusion | bytes 1048640 | tf_op jit(solution)/shard_map/while/body/eval_jaxpr/gather | solution.py:79
  137.0 2.9 %fusion.70 = bf16[4,4,128,2,64]{2,4,3,1,0:T(8,128)(2,1)} fusion(bf16[4,4,128,2,64]{2,4,3,1,0:T(8,128)(2,1)} %get-tuple-element.157, s32[]{:T(128)} %get-tuple-element.156, bf16[4,512,2,64]{3,2,1,0:T(2,128)(2,1)S(1)} %bitcast.77, f32[4,2,128,512]{3,2,1,0:T(8,128)} %get-tuple-element.146, f32[4,2,128]{2,1,0:T(2,128)S(1)} %get-tuple-element.147), kind=kOutput, calls=%fused_computation.10.clone.1 | convolution fusion | flops 68222976 | bytes 2757120 | tf_op jit(solution)/shard_map/while/body/eval_jaxpr/bhij,bjhd->bihd/dot_general | solution.py:85
  140.0 2.7 %gather_fusion.1 = bf16[16,128,2,64]{3,2,1,0:T(2,128)(2,1)S(1)} fusion(bf16[8,128,2,64]{3,2,1,0:T(2,128)(2,1)S(1)} %get-tuple-element.170, s32[1024]{0:T(1024)S(1)} %pad_clamp_fusion.2), kind=kCustom, calls=%fused_computation.1.clone.clone.1 | custom fusion | bytes 1048640 | tf_op jit(solution)/shard_map/while/body/eval_jaxpr/gather | solution.py:78
  142.8 3.1 %fusion.69 = (f32[4,2,128]{2,1,0:T(2,128)S(1)}, f32[4,2,128,512]{3,2,1,0:T(8,128)}) fusion(pred[4,512]{1,0:T(4,128)(4,1)S(1)} %bitcast.83, bf16[4,512,2,64]{3,2,1,0:T(2,128)(2,1)S(1)} %bitcast.76, bf16[4,4,128,2,64]{2,4,3,1,0:T(8,128)(2,1)} %get-tuple-element.169, s32[]{:T(128)} %get-tuple-element.156), kind=kOutput, calls=%fused_computation.51.clone.1 | convolution fusion | flops 69206528 | bytes 2759168 | tf_op jit(solution)/shard_map/while/body/eval_jaxpr/sub | solution.py:15
  145.9 2.7 %gather_fusion = bf16[16,128,2,64]{3,2,1,0:T(2,128)(2,1)S(1)} fusion(bf16[8,128,2,64]{3,2,1,0:T(2,128)(2,1)S(1)} %get-tuple-element.167, s32[1024]{0:T(1024)S(1)} %pad_clamp_fusion.2), kind=kCustom, calls=%fused_computation.clone.clone.1 | custom fusion | bytes 1048640 | tf_op jit(solution)/shard_map/while/body/eval_jaxpr/gather | solution.py:79
  148.6 2.9 %fusion.70 = bf16[4,4,128,2,64]{2,4,3,1,0:T(8,128)(2,1)} fusion(bf16[4,4,128,2,64]{2,4,3,1,0:T(8,128)(2,1)} %get-tuple-element.157, s32[]{:T(128)} %get-tuple-element.156, bf16[4,512,2,64]{3,2,1,0:T(2,128)(2,1)S(1)} %bitcast.77, f32[4,2,128,512]{3,2,1,0:T(8,128)} %get-tuple-element.146, f32[4,2,128]{2,1,0:T(2,128)S(1)} %get-tuple-element.147), kind=kOutput, calls=%fused_computation.10.clone.1 | convolution fusion | flops 68222976 | bytes 2757120 | tf_op jit(solution)/shard_map/while/body/eval_jaxpr/bhij,bjhd->bihd/dot_general | solution.py:85
  151.5 2.4 %copy.35 = bf16[4,4,128,2,64]{4,3,2,1,0:T(2,128)(2,1)S(1)} copy(bf16[4,4,128,2,64]{2,4,3,1,0:T(8,128)(2,1)} %get-tuple-element.47) | data formatting | bytes 1048576 | tf_op jit(solution)/shard_map/while | solution.py:90
  154.3 43.2 %all_to_all.80 = bf16[64,32,128]{2,1,0:T(8,128)(2,1)S(1)} all-to-all(bf16[64,32,128]{2,1,0:T(8,128)(2,1)S(1)} %all_to_all.69), channel_id=1, replica_groups=mesh['grp'=8,'wide'=64] {'wide'}, dimensions={0} | all-to-all | bytes 1048576 | tf_op jit(solution)/shard_map/all_to_all | solution.py:93
  197.6 16.5 %all_to_all.81 = bf16[8,256,128]{2,1,0:T(8,128)(2,1)S(1)} all-to-all(bf16[8,256,128]{2,1,0:T(8,128)(2,1)S(1)} %bitcast.79), channel_id=1, replica_groups=mesh['grp'=8,'wide'=64] {'grp'}, dimensions={0} | all-to-all | bytes 1048576 | tf_op jit(solution)/shard_map/all_to_all | solution.py:92
  215.1 1.6 copy.36
  (65 shorter events, 11.3 us)
Async XLA Ops:
  6.5 210.6 %copy-start = (bf16[1024,512]{1,0:T(8,128)(2,1)S(1)}, bf16[1024,512]{1,0:T(8,128)(2,1)}, u32[]{:S(2)}) copy-start(bf16[1024,512]{1,0:T(8,128)(2,1)} %param.18) | copy-start | bytes 3145732
  6.5 43.6 %all-gather.3.cloned.1.call-start = ((), (), s32[]{:S(2)}) async-start(), calls=%async_computation.6 | async-start | bytes 2359296 | tf_op jit(solution)/shard_map/all_gather | solution.py:44
  7.3 83.8 %all-gather.5.cloned.1.call-start = ((), (), s32[]{:S(2)}) async-start(), calls=%async_computation.7 | async-start | bytes 2359296 | tf_op jit(solution)/shard_map/all_gather | solution.py:43
  8.0 42.1 %copy-start.3 = (bf16[128,1024]{1,0:T(8,128)(2,1)S(1)}, bf16[128,1024]{1,0:T(8,128)(2,1)}, u32[]{:S(2)}) copy-start(bf16[128,1024]{1,0:T(8,128)(2,1)} %param.11) | copy-start | bytes 786436
  9.3 42.9 %copy-start.1 = (bf16[256,1024]{0,1:T(8,128)(2,1)}, bf16[256,1024]{0,1:T(8,128)(2,1)S(1)}, u32[]{:S(2)}) copy-start(bf16[256,1024]{0,1:T(8,128)(2,1)S(1)} %copy.26) | copy-start | bytes 1572868
  29.0 43.9 %all-to-all-start.2 = ((bf16[64,32,128]{2,1,0:T(8,128)(2,1)}), bf16[64,32,128]{2,1,0:T(8,128)(2,1)S(1)}, u32[]{:S(2)}, u32[]{:S(2)}) async-start(bf16[64,32,128]{2,1,0:T(8,128)(2,1)} %bitcast.6), calls=%async_computation.2 | async-start | bytes 1048576 | tf_op jit(solution)/shard_map/all_to_all | solution.py:56
  72.9 25.3 %copy-start.5 = (s32[16,4]{0,1:T(4,128)S(1)}, s32[16,4]{0,1:T(4,128)}, u32[]{:S(2)}) copy-start(s32[16,4]{0,1:T(4,128)} %param.15) | copy-start | bytes 772
  72.9 25.4 %copy-start.6 = (s32[16]{0:T(128)S(1)}, s32[16]{0:T(128)}, u32[]{:S(2)}) copy-start(s32[16]{0:T(128)} %param.16) | copy-start | bytes 196
  72.9 21.0 %all-to-all-start = ((bf16[128,8,128]{0,2,1:T(8,128)(2,1)}), bf16[128,8,128]{0,2,1:T(8,128)(2,1)S(1)}, u32[]{:S(2)}, u32[]{:S(2)}) async-start(bf16[128,8,128]{0,2,1:T(8,128)(2,1)} %bitcast.1), calls=%async_computation | async-start | bytes 524288 | tf_op jit(solution)/shard_map/all_to_all | solution.py:54
  93.9 10.7 %all-to-all-start.3 = ((bf16[128,8,128]{0,2,1:T(8,128)(2,1)}), bf16[128,8,128]{0,2,1:T(8,128)(2,1)S(1)}, u32[]{:S(2)}, u32[]{:S(2)}) async-start(bf16[128,8,128]{0,2,1:T(8,128)(2,1)} %bitcast.7), calls=%async_computation.3 | async-start | bytes 524288 | tf_op jit(solution)/shard_map/all_to_all | solution.py:53
  197.6 19.1 %copy-start.2 = (bf16[256,1024]{0,1:T(8,128)(2,1)S(1)}, bf16[256,1024]{0,1:T(8,128)(2,1)}, u32[]{:S(2)}) copy-start(bf16[256,1024]{0,1:T(8,128)(2,1)} %copy-done.1) | copy-start | bytes 1572868
  215.1 1.8 copy-start.4
  216.7 0.7 copy-start.7
Sparse Core Ops, SparseCore 0:
  9.5 40.6 all-gather.2
  52.2 38.7 all-gather.4
where the time goes:
time: 226 us; the launch traced here: 225 us
  blocking collectives  78.4 us (35%)
  waiting for transfers between devices  41.5 us (18%)
  local copies, waits for them, and re-layouts  33.7 us (15%)
  matrix products  29.3 us (13%)
  starting transfers between devices  27.1 us (12%)
  between operations  13.5 us (6%)
    all_to_all x1, blocking collectives, body(): lax.all_to_all(attended, 'wide', split_axis=0, concat_axis=0, tiled=True)  43.2 us
    all_to_all x1, waiting for transfers between devices, body(): lax.all_to_all(lax.all_to_all(panel_query, 'grp', split_axis=1, concat_ax...  19.9 us
    all_to_all x1, blocking collectives, body(): lax.all_to_all(panel_query, 'grp', split_axis=1, concat_axis=0, tiled=True)  18.6 us
    all_to_all x1, blocking collectives, body(): lax.all_to_all(lax.all_to_all(attended, 'wide', split_axis=0, concat_axis...  16.5 us
    all_to_all x1, starting transfers between devices, body(): lax.all_to_all(lax.all_to_all(panel_query, 'grp', split_axis=1, concat_ax...  14.8 us
    sub x4, matrix products, softmax_rows(): expo = jnp.exp(scores - top)  12.3 us
    dot_general x4, matrix products, attend(): jnp.einsum('bhij,bjhd->bihd', weights, picked_values, preferred_element_t...  11.7 us
    gather x4, local copies, waits for them, and re-layouts, attend(): key_blocks[listed].reshape(per_step, LMAX * BLK, local_heads, HD)  10.6 us
  transfers between devices with their start and end apart: 5, of which 4 were waited for; matrix products, arithmetic and copies ran while one was open for 5% of the time, Pallas kernels for 0%

commit v1 on v0

--- a/solution.py
+++ b/solution.py
@@ -1,3 +1,4 @@
+import functools
 import math
 import jax
 import jax.numpy as jnp
@@ -7,6 +8,17 @@
 BLK = 128
 LMAX = 4
 HD = 64
+
+
+def positions_cut(slab_in, net_axis):
+    u1 = jax.lax.psum(1, net_axis)
+    wide_out = jnp.stack(u1 * [slab_in])
+    e_now = jax.lax.all_to_all(wide_out, net_axis, 0, 0)
+    block_now = jnp.concatenate(e_now, axis=1)
+    return block_now
+
+
+feed_pages = functools.partial(positions_cut, net_axis="grp")
 
 
 def softmax_rows(scores, mask):
@@ -40,7 +52,7 @@
     flux_weight,
 ):
     full_keys_w, full_values_w = (
-        lax.all_gather(key_weight, "grp", axis=1, tiled=True),
+        feed_pages(key_weight),
         lax.all_gather(value_weight, "grp", axis=1, tiled=True),
     )
     local_keys = jnp.dot(anchor_states, full_keys_w, preferred_element_type=jnp.float32).astype(

time: 226 us -> 245 us (1.084)
  blocking collectives: 78.4 us -> 50.9 us
  waiting for transfers between devices: 41.5 us -> 67 us
  starting transfers between devices: 27.1 us -> 42.6 us
  local copies, waits for them, and re-layouts: 33.7 us -> 39.2 us
    all_to_all x0 -> x2, waiting for transfers between devices: none -> 31.8 us  [the longest x1 25.5 us: positions_cut(): e_now = jax.lax.all_to_all(wide_out, net_axis, 0, 0)]
    all_to_all x1 -> x0, blocking collectives: 18.6 us -> none  [body(): lax.all_to_all(panel_query, 'grp', split_axis=1, concat_axis=0, tiled=True)]
    all_to_all x0 -> x2, starting transfers between devices: none -> 16.2 us  [the longest x1 10.4 us: positions_cut(): e_now = jax.lax.all_to_all(wide_out, net_axis, 0, 0)]
    all_gather x1 -> x0, waiting for transfers between devices: 10.1 us -> none  [body(): lax.all_gather(key_weight, 'grp', axis=1, tiled=True)]
    all_to_all x1, blocking collectives: 43.2 us -> 34.5 us  [body(): lax.all_to_all(attended, 'wide', split_axis=0, concat_axis=0, tiled=True)]
    all_gather x1, waiting for transfers between devices: 6.39 us -> 0.02 us  [body(): lax.all_gather(value_weight, 'grp', axis=1, tiled=True)]
    all_to_all x1, waiting for transfers between devices: 19.9 us -> 26.2 us  [body(): lax.all_to_all(lax.all_to_all(panel_query, 'grp', split_axis=1, concat_ax...]
    all_to_all x1, waiting for transfers between devices: 0.01 us -> 3.78 us  [body(): lax.all_to_all(local_values, 'grp', split_axis=1, concat_axis=0, tiled=True)]
  transfers between devices with their start and end apart: 5 -> 6, of which waited for: 4 -> 5; matrix products, arithmetic and copies ran while one was open for 5% -> 5% of each run, Pallas kernels for 0% -> 0%
where the time goes in v1:
time: 245 us; the launch traced here: 244 us
  waiting for transfers between devices  67 us (27%)
  blocking collectives  50.9 us (21%)
  starting transfers between devices  42.6 us (17%)
  local copies, waits for them, and re-layouts  39.2 us (16%)
  matrix products  28.8 us (12%)
  between operations  13.5 us (6%)
    all_to_all x1, blocking collectives, body(): lax.all_to_all(attended, 'wide', split_axis=0, concat_axis=0, tiled=True)  34.5 us
    all_to_all x1, waiting for transfers between devices, body(): lax.all_to_all(lax.all_to_all(panel_query, 'grp', split_axis=1, concat_ax...  26.2 us
    all_to_all x1, waiting for transfers between devices, positions_cut(): e_now = jax.lax.all_to_all(wide_out, net_axis, 0, 0)  25.5 us
    all_to_all x1, blocking collectives, body(): lax.all_to_all(lax.all_to_all(attended, 'wide', split_axis=0, concat_axis...  16.4 us
    all_to_all x1, starting transfers between devices, body(): lax.all_to_all(lax.all_to_all(panel_query, 'grp', split_axis=1, concat_ax...  12.7 us
    sub x4, matrix products, softmax_rows(): expo = jnp.exp(scores - top)  12.3 us
    dot_general x4, matrix products, attend(): jnp.einsum('bhij,bjhd->bihd', weights, picked_values, preferred_element_t...  11.7 us
    gather x4, local copies, waits for them, and re-layouts, attend(): key_blocks[listed].reshape(per_step, LMAX * BLK, local_heads, HD)  10.6 us
  transfers between devices with their start and end apart: 6, of which 5 were waited for; matrix products, arithmetic and copies ran while one was open for 5% of the time, Pallas kernels for 0%

profile of v1, /device:TPU:1, one launch (start us, length us, event | category | flops | bytes accessed | tf_op | source)
XLA Modules:
  0.0 244.0 jit_solution(16383794095079255475)
XLA Ops:
  9.3 10.4 %all-to-all-start.3 = ((bf16[8,1024,128]{1,2,0:T(8,128)(2,1)}), bf16[8,1024,128]{1,2,0:T(8,128)(2,1)S(1)}, u32[]{:S(2)}, u32[]{:S(2)}) async-start(bf16[8,1024,128]{1,2,0:T(8,128)(2,1)} %stack.2), calls=%async_computation.3 | async-start | bytes 4194304 | tf_op jit(solution)/shard_map/all_to_all | solution.py:16
  20.4 2.0 copy.27
  22.4 25.5 %all-to-all-done.3 = bf16[8,1024,128]{1,2,0:T(8,128)(2,1)S(1)} async-done(((bf16[8,1024,128]{1,2,0:T(8,128)(2,1)}), bf16[8,1024,128]{1,2,0:T(8,128)(2,1)S(1)}, u32[]{:S(2)}, u32[]{:S(2)}) %all-to-all-start.3) | async-done | bytes 2097184 | tf_op jit(solution)/shard_map/all_to_all | solution.py:16
  48.0 5.8 %all-to-all-start.1 = ((bf16[256,8,128]{0,2,1:T(8,128)(2,1)}), bf16[256,8,128]{0,2,1:T(8,128)(2,1)}, u32[]{:S(2)}, u32[]{:S(2)}) async-start(bf16[256,8,128]{0,2,1:T(8,128)(2,1)} %bitcast.82), calls=%async_computation.1 | async-start | bytes 1048576 | tf_op jit(solution)/shard_map/all_to_all | solution.py:69
  57.1 6.3 %all-to-all-done.1 = bf16[256,8,128]{0,2,1:T(8,128)(2,1)} async-done(((bf16[256,8,128]{0,2,1:T(8,128)(2,1)}), bf16[256,8,128]{0,2,1:T(8,128)(2,1)}, u32[]{:S(2)}, u32[]{:S(2)}) %all-to-all-start.1) | async-done | bytes 524320 | tf_op jit(solution)/shard_map/all_to_all | solution.py:69
  63.3 5.9 %all-to-all-start.4 = ((bf16[128,8,128]{0,2,1:T(8,128)(2,1)}), bf16[128,8,128]{0,2,1:T(8,128)(2,1)S(1)}, u32[]{:S(2)}, u32[]{:S(2)}) async-start(bf16[128,8,128]{0,2,1:T(8,128)(2,1)} %bitcast.9), calls=%async_computation.4 | async-start | bytes 524288 | tf_op jit(solution)/shard_map/all_to_all | solution.py:65
  69.2 2.1 copy.30
  71.3 4.5 %all-to-all-done.4 = bf16[128,8,128]{0,2,1:T(8,128)(2,1)S(1)} async-done(((bf16[128,8,128]{0,2,1:T(8,128)(2,1)}), bf16[128,8,128]{0,2,1:T(8,128)(2,1)S(1)}, u32[]{:S(2)}, u32[]{:S(2)}) %all-to-all-start.4) | async-done | bytes 262176 | tf_op jit(solution)/shard_map/all_to_all | solution.py:65
  75.7 12.7 %all-to-all-start.2 = ((bf16[64,32,128]{2,1,0:T(8,128)(2,1)}), bf16[64,32,128]{2,1,0:T(8,128)(2,1)S(1)}, u32[]{:S(2)}, u32[]{:S(2)}) async-start(bf16[64,32,128]{2,1,0:T(8,128)(2,1)} %bitcast.6), calls=%async_computation.2 | async-start | bytes 1048576 | tf_op jit(solution)/shard_map/all_to_all | solution.py:68
  91.3 26.2 %all-to-all-done.2 = bf16[64,32,128]{2,1,0:T(8,128)(2,1)S(1)} async-done(((bf16[64,32,128]{2,1,0:T(8,128)(2,1)}), bf16[64,32,128]{2,1,0:T(8,128)(2,1)S(1)}, u32[]{:S(2)}, u32[]{:S(2)}) %all-to-all-start.2) | async-done | bytes 524320 | tf_op jit(solution)/shard_map/all_to_all | solution.py:68
  117.5 7.9 %all-to-all-start = ((bf16[128,8,128]{0,2,1:T(8,128)(2,1)}), bf16[128,8,128]{0,2,1:T(8,128)(2,1)S(1)}, u32[]{:S(2)}, u32[]{:S(2)}) async-start(bf16[128,8,128]{0,2,1:T(8,128)(2,1)} %bitcast.1), calls=%async_computation | async-start | bytes 524288 | tf_op jit(solution)/shard_map/all_to_all | solution.py:66
  128.2 3.8 %all-to-all-done = bf16[128,8,128]{0,2,1:T(8,128)(2,1)S(1)} async-done(((bf16[128,8,128]{0,2,1:T(8,128)(2,1)}), bf16[128,8,128]{0,2,1:T(8,128)(2,1)S(1)}, u32[]{:S(2)}, u32[]{:S(2)}) %all-to-all-start) | async-done | bytes 262176 | tf_op jit(solution)/shard_map/all_to_all | solution.py:66
  132.4 46.4 %while.11 = (s32[]{:T(128)}, bf16[4,4,128,2,64]{2,4,3,1,0:T(8,128)(2,1)}, s32[4,4,4]{2,1,0:T(4,128)S(1)}, bf16[8,128,2,64]{3,2,1,0:T(2,128)(2,1)S(1)}, s32[4,4]{...) while((s32[]{:T(128)}, ...), condition=%wide.region_3.4_spmd.clone, body=%wide.region_0.3_spmd.clone.sunk | while | flops 137430592 | bytes 7624301 | solution.py:102
  132.5 2.7 %gather_fusion.1 = bf16[16,128,2,64]{3,2,1,0:T(2,128)(2,1)S(1)} fusion(bf16[8,128,2,64]{3,2,1,0:T(2,128)(2,1)S(1)} %get-tuple-element.170, s32[1024]{0:T(1024)S(1)} %pad_clamp_fusion.2), kind=kCustom, calls=%fused_computation.1.clone.clone.1 | custom fusion | bytes 1048640 | tf_op jit(solution)/shard_map/while/body/eval_jaxpr/gather | solution.py:90
  135.4 3.1 %fusion.69 = (f32[4,2,128]{2,1,0:T(2,128)S(1)}, f32[4,2,128,512]{3,2,1,0:T(8,128)}) fusion(pred[4,512]{1,0:T(4,128)(4,1)S(1)} %bitcast.86, bf16[4,512,2,64]{3,2,1,0:T(2,128)(2,1)S(1)} %bitcast.79, bf16[4,4,128,2,64]{2,4,3,1,0:T(8,128)(2,1)} %get-tuple-element.169, s32[]{:T(128)} %get-tuple-element.156), kind=kOutput, calls=%fused_computation.51.clone.1 | convolution fusion | flops 69206528 | bytes 2759168 | tf_op jit(solution)/shard_map/while/body/eval_jaxpr/sub | solution.py:27
  138.4 2.7 %gather_fusion = bf16[16,128,2,64]{3,2,1,0:T(2,128)(2,1)S(1)} fusion(bf16[8,128,2,64]{3,2,1,0:T(2,128)(2,1)S(1)} %get-tuple-element.167, s32[1024]{0:T(1024)S(1)} %pad_clamp_fusion.2), kind=kCustom, calls=%fused_computation.clone.clone.1 | custom fusion | bytes 1048640 | tf_op jit(solution)/shard_map/while/body/eval_jaxpr/gather | solution.py:91
  141.1 2.9 %fusion.70 = bf16[4,4,128,2,64]{2,4,3,1,0:T(8,128)(2,1)} fusion(bf16[4,4,128,2,64]{2,4,3,1,0:T(8,128)(2,1)} %get-tuple-element.157, s32[]{:T(128)} %get-tuple-element.156, bf16[4,512,2,64]{3,2,1,0:T(2,128)(2,1)S(1)} %bitcast.80, f32[4,2,128,512]{3,2,1,0:T(8,128)} %get-tuple-element.146, f32[4,2,128]{2,1,0:T(2,128)S(1)} %get-tuple-element.147), kind=kOutput, calls=%fused_computation.10.clone.1 | convolution fusion | flops 68222976 | bytes 2757120 | tf_op jit(solution)/shard_map/while/body/eval_jaxpr/bhij,bjhd->bihd/dot_general | solution.py:97
  144.1 2.7 %gather_fusion.1 = bf16[16,128,2,64]{3,2,1,0:T(2,128)(2,1)S(1)} fusion(bf16[8,128,2,64]{3,2,1,0:T(2,128)(2,1)S(1)} %get-tuple-element.170, s32[1024]{0:T(1024)S(1)} %pad_clamp_fusion.2), kind=kCustom, calls=%fused_computation.1.clone.clone.1 | custom fusion | bytes 1048640 | tf_op jit(solution)/shard_map/while/body/eval_jaxpr/gather | solution.py:90
  146.9 3.1 %fusion.69 = (f32[4,2,128]{2,1,0:T(2,128)S(1)}, f32[4,2,128,512]{3,2,1,0:T(8,128)}) fusion(pred[4,512]{1,0:T(4,128)(4,1)S(1)} %bitcast.86, bf16[4,512,2,64]{3,2,1,0:T(2,128)(2,1)S(1)} %bitcast.79, bf16[4,4,128,2,64]{2,4,3,1,0:T(8,128)(2,1)} %get-tuple-element.169, s32[]{:T(128)} %get-tuple-element.156), kind=kOutput, calls=%fused_computation.51.clone.1 | convolution fusion | flops 69206528 | bytes 2759168 | tf_op jit(solution)/shard_map/while/body/eval_jaxpr/sub | solution.py:27
  150.0 2.7 %gather_fusion = bf16[16,128,2,64]{3,2,1,0:T(2,128)(2,1)S(1)} fusion(bf16[8,128,2,64]{3,2,1,0:T(2,128)(2,1)S(1)} %get-tuple-element.167, s32[1024]{0:T(1024)S(1)} %pad_clamp_fusion.2), kind=kCustom, calls=%fused_computation.clone.clone.1 | custom fusion | bytes 1048640 | tf_op jit(solution)/shard_map/while/body/eval_jaxpr/gather | solution.py:91
  152.7 2.9 %fusion.70 = bf16[4,4,128,2,64]{2,4,3,1,0:T(8,128)(2,1)} fusion(bf16[4,4,128,2,64]{2,4,3,1,0:T(8,128)(2,1)} %get-tuple-element.157, s32[]{:T(128)} %get-tuple-element.156, bf16[4,512,2,64]{3,2,1,0:T(2,128)(2,1)S(1)} %bitcast.80, f32[4,2,128,512]{3,2,1,0:T(8,128)} %get-tuple-element.146, f32[4,2,128]{2,1,0:T(2,128)S(1)} %get-tuple-element.147), kind=kOutput, calls=%fused_computation.10.clone.1 | convolution fusion | flops 68222976 | bytes 2757120 | tf_op jit(solution)/shard_map/while/body/eval_jaxpr/bhij,bjhd->bihd/dot_general | solution.py:97
  155.7 2.7 %gather_fusion.1 = bf16[16,128,2,64]{3,2,1,0:T(2,128)(2,1)S(1)} fusion(bf16[8,128,2,64]{3,2,1,0:T(2,128)(2,1)S(1)} %get-tuple-element.170, s32[1024]{0:T(1024)S(1)} %pad_clamp_fusion.2), kind=kCustom, calls=%fused_computation.1.clone.clone.1 | custom fusion | bytes 1048640 | tf_op jit(solution)/shard_map/while/body/eval_jaxpr/gather | solution.py:90
  158.6 3.1 %fusion.69 = (f32[4,2,128]{2,1,0:T(2,128)S(1)}, f32[4,2,128,512]{3,2,1,0:T(8,128)}) fusion(pred[4,512]{1,0:T(4,128)(4,1)S(1)} %bitcast.86, bf16[4,512,2,64]{3,2,1,0:T(2,128)(2,1)S(1)} %bitcast.79, bf16[4,4,128,2,64]{2,4,3,1,0:T(8,128)(2,1)} %get-tuple-element.169, s32[]{:T(128)} %get-tuple-element.156), kind=kOutput, calls=%fused_computation.51.clone.1 | convolution fusion | flops 69206528 | bytes 2759168 | tf_op jit(solution)/shard_map/while/body/eval_jaxpr/sub | solution.py:27
  161.6 2.7 %gather_fusion = bf16[16,128,2,64]{3,2,1,0:T(2,128)(2,1)S(1)} fusion(bf16[8,128,2,64]{3,2,1,0:T(2,128)(2,1)S(1)} %get-tuple-element.167, s32[1024]{0:T(1024)S(1)} %pad_clamp_fusion.2), kind=kCustom, calls=%fused_computation.clone.clone.1 | custom fusion | bytes 1048640 | tf_op jit(solution)/shard_map/while/body/eval_jaxpr/gather | solution.py:91
  164.3 2.9 %fusion.70 = bf16[4,4,128,2,64]{2,4,3,1,0:T(8,128)(2,1)} fusion(bf16[4,4,128,2,64]{2,4,3,1,0:T(8,128)(2,1)} %get-tuple-element.157, s32[]{:T(128)} %get-tuple-element.156, bf16[4,512,2,64]{3,2,1,0:T(2,128)(2,1)S(1)} %bitcast.80, f32[4,2,128,512]{3,2,1,0:T(8,128)} %get-tuple-element.146, f32[4,2,128]{2,1,0:T(2,128)S(1)} %get-tuple-element.147), kind=kOutput, calls=%fused_computation.10.clone.1 | convolution fusion | flops 68222976 | bytes 2757120 | tf_op jit(solution)/shard_map/while/body/eval_jaxpr/bhij,bjhd->bihd/dot_general | solution.py:97
  167.3 2.7 %gather_fusion.1 = bf16[16,128,2,64]{3,2,1,0:T(2,128)(2,1)S(1)} fusion(bf16[8,128,2,64]{3,2,1,0:T(2,128)(2,1)S(1)} %get-tuple-element.170, s32[1024]{0:T(1024)S(1)} %pad_clamp_fusion.2), kind=kCustom, calls=%fused_computation.1.clone.clone.1 | custom fusion | bytes 1048640 | tf_op jit(solution)/shard_map/while/body/eval_jaxpr/gather | solution.py:90
  170.2 3.1 %fusion.69 = (f32[4,2,128]{2,1,0:T(2,128)S(1)}, f32[4,2,128,512]{3,2,1,0:T(8,128)}) fusion(pred[4,512]{1,0:T(4,128)(4,1)S(1)} %bitcast.86, bf16[4,512,2,64]{3,2,1,0:T(2,128)(2,1)S(1)} %bitcast.79, bf16[4,4,128,2,64]{2,4,3,1,0:T(8,128)(2,1)} %get-tuple-element.169, s32[]{:T(128)} %get-tuple-element.156), kind=kOutput, calls=%fused_computation.51.clone.1 | convolution fusion | flops 69206528 | bytes 2759168 | tf_op jit(solution)/shard_map/while/body/eval_jaxpr/sub | solution.py:27
  173.2 2.7 %gather_fusion = bf16[16,128,2,64]{3,2,1,0:T(2,128)(2,1)S(1)} fusion(bf16[8,128,2,64]{3,2,1,0:T(2,128)(2,1)S(1)} %get-tuple-element.167, s32[1024]{0:T(1024)S(1)} %pad_clamp_fusion.2), kind=kCustom, calls=%fused_computation.clone.clone.1 | custom fusion | bytes 1048640 | tf_op jit(solution)/shard_map/while/body/eval_jaxpr/gather | solution.py:91
  175.9 2.9 %fusion.70 = bf16[4,4,128,2,64]{2,4,3,1,0:T(8,128)(2,1)} fusion(bf16[4,4,128,2,64]{2,4,3,1,0:T(8,128)(2,1)} %get-tuple-element.157, s32[]{:T(128)} %get-tuple-element.156, bf16[4,512,2,64]{3,2,1,0:T(2,128)(2,1)S(1)} %bitcast.80, f32[4,2,128,512]{3,2,1,0:T(8,128)} %get-tuple-element.146, f32[4,2,128]{2,1,0:T(2,128)S(1)} %get-tuple-element.147), kind=kOutput, calls=%fused_computation.10.clone.1 | convolution fusion | flops 68222976 | bytes 2757120 | tf_op jit(solution)/shard_map/while/body/eval_jaxpr/bhij,bjhd->bihd/dot_general | solution.py:97
  178.8 2.4 copy.37
  181.7 34.5 %all_to_all.84 = bf16[64,32,128]{2,1,0:T(8,128)(2,1)S(1)} all-to-all(bf16[64,32,128]{2,1,0:T(8,128)(2,1)S(1)} %all_to_all.73), channel_id=1, replica_groups=mesh['grp'=8,'wide'=64] {'wide'}, dimensions={0} | all-to-all | bytes 1048576 | tf_op jit(solution)/shard_map/all_to_all | solution.py:105
  216.2 16.4 %all_to_all.85 = bf16[8,256,128]{2,1,0:T(8,128)(2,1)S(1)} all-to-all(bf16[8,256,128]{2,1,0:T(8,128)(2,1)S(1)} %bitcast.83), channel_id=1, replica_groups=mesh['grp'=8,'wide'=64] {'grp'}, dimensions={0} | all-to-all | bytes 1048576 | tf_op jit(solution)/shard_map/all_to_all | solution.py:104
  (65 shorter events, 18.9 us)
Async XLA Ops:
  6.5 229.1 %copy-start = (bf16[1024,512]{1,0:T(8,128)(2,1)S(1)}, bf16[1024,512]{1,0:T(8,128)(2,1)}, u32[]{:S(2)}) copy-start(bf16[1024,512]{1,0:T(8,128)(2,1)} %param.18) | copy-start | bytes 3145732
  9.3 38.7 %all-to-all-start.3 = ((bf16[8,1024,128]{1,2,0:T(8,128)(2,1)}), bf16[8,1024,128]{1,2,0:T(8,128)(2,1)S(1)}, u32[]{:S(2)}, u32[]{:S(2)}) async-start(bf16[8,1024,128]{1,2,0:T(8,128)(2,1)} %stack.2), calls=%async_computation.3 | async-start | bytes 4194304 | tf_op jit(solution)/shard_map/all_to_all | solution.py:16
  19.7 34.1 %copy-start.2 = (bf16[128,1024]{1,0:T(8,128)(2,1)S(1)}, bf16[128,1024]{1,0:T(8,128)(2,1)}, u32[]{:S(2)}) copy-start(bf16[128,1024]{1,0:T(8,128)(2,1)} %param.11) | copy-start | bytes 786436
  19.7 68.8 %all-gather.2.cloned.1.call-start = ((), (), s32[]{:S(2)}) async-start(), calls=%async_computation.7 | async-start | bytes 2359296 | tf_op jit(solution)/shard_map/all_gather | solution.py:56
  48.0 15.4 %all-to-all-start.1 = ((bf16[256,8,128]{0,2,1:T(8,128)(2,1)}), bf16[256,8,128]{0,2,1:T(8,128)(2,1)}, u32[]{:S(2)}, u32[]{:S(2)}) async-start(bf16[256,8,128]{0,2,1:T(8,128)(2,1)} %bitcast.82), calls=%async_computation.1 | async-start | bytes 1048576 | tf_op jit(solution)/shard_map/all_to_all | solution.py:69
  63.3 12.4 %all-to-all-start.4 = ((bf16[128,8,128]{0,2,1:T(8,128)(2,1)}), bf16[128,8,128]{0,2,1:T(8,128)(2,1)S(1)}, u32[]{:S(2)}, u32[]{:S(2)}) async-start(bf16[128,8,128]{0,2,1:T(8,128)(2,1)} %bitcast.9), calls=%async_computation.4 | async-start | bytes 524288 | tf_op jit(solution)/shard_map/all_to_all | solution.py:65
  75.7 41.8 %all-to-all-start.2 = ((bf16[64,32,128]{2,1,0:T(8,128)(2,1)}), bf16[64,32,128]{2,1,0:T(8,128)(2,1)S(1)}, u32[]{:S(2)}, u32[]{:S(2)}) async-start(bf16[64,32,128]{2,1,0:T(8,128)(2,1)} %bitcast.6), calls=%async_computation.2 | async-start | bytes 1048576 | tf_op jit(solution)/shard_map/all_to_all | solution.py:68
  88.4 37.1 %copy-start.4 = (s32[16,4]{0,1:T(4,128)S(1)}, s32[16,4]{0,1:T(4,128)}, u32[]{:S(2)}) copy-start(s32[16,4]{0,1:T(4,128)} %param.15) | copy-start | bytes 772
  88.4 37.2 %copy-start.5 = (s32[16]{0:T(128)S(1)}, s32[16]{0:T(128)}, u32[]{:S(2)}) copy-start(s32[16]{0:T(128)} %param.16) | copy-start | bytes 196
  117.5 14.5 %all-to-all-start = ((bf16[128,8,128]{0,2,1:T(8,128)(2,1)}), bf16[128,8,128]{0,2,1:T(8,128)(2,1)S(1)}, u32[]{:S(2)}, u32[]{:S(2)}) async-start(bf16[128,8,128]{0,2,1:T(8,128)(2,1)} %bitcast.1), calls=%async_computation | async-start | bytes 524288 | tf_op jit(solution)/shard_map/all_to_all | solution.py:66
  232.5 2.6 %copy-start.1 = (bf16[256,1024]{0,1:T(8,128)(2,1)S(1)}, bf16[256,1024]{0,1:T(8,128)(2,1)}, u32[]{:S(2)}) copy-start(bf16[256,1024]{0,1:T(8,128)(2,1)} %copy.27) | copy-start | bytes 1572868
  233.6 1.8 copy-start.3
  235.2 0.7 copy-start.6
Sparse Core Ops, SparseCore 0:
  22.6 41.3 all-gather.1
